TPU v7x, 32 devices: a whole 2x2x4 slice. The times are simulated.
32 devices in a mesh: grp: 2 (over y), tm: 8 (over z, x), sens: 2 (over core).
Axes of the slice: x: 2, y: 2, z: 4, core: 2. Of those that a mesh axis runs over, the one named last changes fastest.
Arguments:
- features: bfloat16 [256, 2048, 128], P(('grp', 'sens'), 'tm'), parts along dimension 0, may hold values from -6 to 6
- target: float32 [256, 2048], P(('grp', 'sens'), 'tm'), parts along dimension 0, may hold values from -60 to 60
- test_matrix: float32 [2048, 64], P('tm'), may hold values from -0.125 to 0.125
- leading_conv_taps: bfloat16 [3, 2, 128, 128], replicated, may hold values from -0.375 to 0.375
- trailing_conv_taps: bfloat16 [3, 2, 128, 128], replicated, may hold values from -0.375 to 0.375
- readout: bfloat16 [128], replicated, may hold values from -0.5 to 0.5
- dilations: int32 [3], replicated, may hold values from 1 to 128, as said below
Outputs:
- remainder: float32 [256, 2048], P(('grp', 'sens'), 'tm'), parts along dimension 0
There are 2 independent parts, one for each index of `grp`. A program takes and returns all parts, laid end to end along the dimension named above; an argument that names none is the same for every part. Nothing has to cross between parts.
Inputs may be any that keep to these rules, and one draw needn't show every extreme that they name: `dilations`: every dilation is a power of two, and the last block has dilation exactly 128.
All inputs are finite; a program needn't handle non-finite values.
Results may differ from a plain program's by a relative error of at most 0.0056.
Values may be sent and summed in bfloat16 or wider, within the bound.
A program may use at most 64 MiB of HBM per device.

v0:
```python
import jax
import jax.numpy as jnp
from jax import lax
from jax.sharding import PartitionSpec as P

LAYERS = 3
DMAX = 128


def shifted(value, axis, by):
    peers = lax.axis_size(axis)
    pairs = [(i, i + by) for i in range(peers) if 0 <= i + by < peers]
    return lax.ppermute(value, axis, pairs)


def dilated(before, current, dist, weight):
    extended = jnp.concatenate([before, current], axis=1)
    moved = lax.dynamic_slice_in_dim(extended, before.shape[1] - dist, current.shape[1], 1)
    total = jnp.einsum("stc,cd->std", moved, weight[0], preferred_element_type=jnp.float32)
    return total + jnp.einsum("stc,cd->std", current, weight[1], preferred_element_type=jnp.float32)


def causal_tail(value):
    return shifted(value[:, -DMAX:, :], "tm", 1)


def time_total(value):
    return lax.psum(value, "tm")


def joint_total(cross, sketch):
    return lax.psum((cross, jnp.dot(sketch.T, sketch, precision=lax.Precision.HIGHEST)), "sens")


def lower_solve(factor, value):
    return jax.scipy.linalg.solve_triangular(factor, value, lower=True)


def on_device(
    features, target, test_matrix, leading_conv_taps, trailing_conv_taps, readout, dilations
):
    hidden = features
    for layer in range(LAYERS):
        dist = dilations[layer]
        inner = jax.nn.relu(
            dilated(causal_tail(hidden), hidden, dist, leading_conv_taps[layer])
        ).astype(jnp.bfloat16)
        branch = jax.nn.relu(dilated(causal_tail(inner), inner, dist, trailing_conv_taps[layer]))
        hidden = (hidden.astype(jnp.float32) + branch).astype(jnp.bfloat16)
    prediction_values = jnp.einsum("stc,c->st", hidden, readout, preferred_element_type=jnp.float32)
    resid = target - prediction_values
    high = lax.Precision.HIGHEST
    sketch = time_total(jnp.dot(resid, test_matrix, precision=high))
    cross, gram = joint_total(jnp.dot(resid.T, sketch, precision=high), sketch)
    factor = jnp.linalg.cholesky(gram)
    projected = lower_solve(factor, cross.T).T
    sketch_two = time_total(jnp.dot(resid, projected, precision=high))
    cross_two, gram_two = joint_total(jnp.dot(sketch_two.T, resid, precision=high), sketch_two)
    factor_two = jnp.linalg.cholesky(gram_two)
    coef = lower_solve(factor_two, cross_two)
    basis_two = lower_solve(factor_two, sketch_two.T).T
    return resid - jnp.dot(basis_two, coef, precision=high)


def solution(mesh):
    placed = (
        P(("grp", "sens"), "tm", None),
        P(("grp", "sens"), "tm"),
        P("tm", None),
        P(),
        P(),
        P(),
        P(),
    )
    return jax.shard_map(
        on_device, mesh=mesh, in_specs=placed, out_specs=P(("grp", "sens"), "tm"), check_vma=False
    )
```

profile of v0, /device:TPU:0, one launch (start us, length us, event | category | flops | bytes accessed | tf_op | source)
XLA Modules:
  0.0 487.6 jit_solution(818690445789708365)
XLA Ops:
  8.3 6.3 %collective-permute-start = (bf16[64,128,128]{2,1,0:T(8,128)(2,1)S(1)}, bf16[64,128,128]{2,1,0:T(8,128)(2,1)}, u32[]{:S(2)}, u32[]{:S(2)}) collective-permute-start(bf16[64,128,128]{2,1,0:T(8,128)(2,1)S(1)} %slice.107), channel_id=1, source_target_pairs={{0,2},{2,4},{4,6},{6,8},{8,10},{10,12},{12,14},{1,3},{3,5},{5,7},{... | collective-permute-start | bytes 6291464 | tf_op jit(solution)/shard_map/ppermute | solution.py:13
  16.6 6.8 %fusion.48 = f32[64,256,128]{2,1,0:T(8,128)} fusion(bf16[64,256,128]{2,1,0:T(8,128)(2,1)} %param.10, bf16[3,2,128,128]{3,2,1,0:T(8,128)(2,1)S(1)} %copy-done.7), kind=kOutput, calls=%fused_computation.52 | convolution fusion | flops 536870912 | bytes 12615680 | tf_op jit(solution)/shard_map/stc,cd->std/dot_general | solution.py:20
  23.4 34.7 %collective-permute-done = bf16[64,128,128]{2,1,0:T(8,128)(2,1)} collective-permute-done((bf16[64,128,128]{2,1,0:T(8,128)(2,1)S(1)}, bf16[64,128,128]{2,1,0:T(8,128)(2,1)}, u32[]{:S(2)}, u32[]{:S(2)}) %collective-permute-start) | collective-permute-done | bytes 2097184 | tf_op jit(solution)/shard_map/ppermute | solution.py:13
  58.1 6.4 %maximum_convert_fusion.2 = bf16[64,256,128]{2,1,0:T(8,128)(2,1)S(1)} fusion(f32[64,256,128]{2,1,0:T(8,128)} %fusion.48, s32[]{:T(128)S(6)} %select_n.15, bf16[64,128,128]{2,1,0:T(8,128)(2,1)} %collective-permute-done, bf16[64,256,128]{2,1,0:T(8,128)(2,1)S(1)} %copy-done.5, bf16[3,2,128,128]{3,2,1,0:T(8,128)(2,1)S(1)} %copy-done.7), kind=kOutput, calls=%fused_computation.5 | convolution fusion | flops 551550976 | bytes 18907140 | tf_op jit(solution)/shard_map/stc,cd->std/dot_general | solution.py:19
  64.7 4.6 collective-permute-start.1
  69.4 4.5 fusion.45
  73.8 39.4 %collective-permute-done.1 = bf16[64,128,128]{2,1,0:T(8,128)(2,1)S(1)} collective-permute-done((bf16[64,128,128]{2,1,0:T(8,128)(2,1)S(1)}, bf16[64,128,128]{2,1,0:T(8,128)(2,1)S(1)}, u32[]{:S(2)}, u32[]{:S(2)}) %collective-permute-start.1) | collective-permute-done | bytes 2097184 | tf_op jit(solution)/shard_map/ppermute | solution.py:13
  113.2 5.9 %add_convert_fusion.2 = bf16[64,256,128]{2,1,0:T(8,128)(2,1)S(1)} fusion(f32[64,256,128]{2,1,0:T(8,128)} %fusion.45, bf16[64,256,128]{2,1,0:T(8,128)(2,1)S(1)} %copy-done.5, s32[]{:T(128)S(6)} %select_n.15, bf16[64,128,128]{2,1,0:T(8,128)(2,1)S(1)} %collective-permute-done.1, bf16[64,256,128]{2,1,0:T(8,128)(2,1)S(1)} %maximum_convert_fusion.2, ...), kind=kOutput, calls=%fused_computation.4 | convolution fusion | flops 555745280 | bytes 23101444 | tf_op jit(solution)/shard_map/stc,cd->std/dot_general | solution.py:19
  121.3 5.8 %collective-permute-start.2 = (bf16[64,128,128]{2,1,0:T(8,128)(2,1)S(1)}, bf16[64,128,128]{2,1,0:T(8,128)(2,1)}, u32[]{:S(2)}, u32[]{:S(2)}) collective-permute-start(bf16[64,128,128]{2,1,0:T(8,128)(2,1)S(1)} %slice.129), channel_id=1, source_target_pairs={{0,2},{2,4},{4,6},{6,8},{8,10},{10,12},{12,14},{1,3},{3,5},{5,7},{... | collective-permute-start | bytes 6291464 | tf_op jit(solution)/shard_map/ppermute | solution.py:13
  128.3 6.8 %fusion.42 = f32[64,256,128]{2,1,0:T(8,128)} fusion(bf16[64,256,128]{2,1,0:T(8,128)(2,1)} %copy-done.3, bf16[3,2,128,128]{3,2,1,0:T(8,128)(2,1)S(1)} %copy-done.7), kind=kOutput, calls=%fused_computation.46 | convolution fusion | flops 536870912 | bytes 12615680 | tf_op jit(solution)/shard_map/stc,cd->std/dot_general | solution.py:20
  135.1 33.7 %collective-permute-done.2 = bf16[64,128,128]{2,1,0:T(8,128)(2,1)} collective-permute-done((bf16[64,128,128]{2,1,0:T(8,128)(2,1)S(1)}, bf16[64,128,128]{2,1,0:T(8,128)(2,1)}, u32[]{:S(2)}, u32[]{:S(2)}) %collective-permute-start.2) | collective-permute-done | bytes 2097184 | tf_op jit(solution)/shard_map/ppermute | solution.py:13
  168.8 6.4 %maximum_convert_fusion.1 = bf16[64,256,128]{2,1,0:T(8,128)(2,1)S(1)} fusion(f32[64,256,128]{2,1,0:T(8,128)} %fusion.42, s32[]{:T(128)S(6)} %select_n.16, bf16[64,128,128]{2,1,0:T(8,128)(2,1)} %collective-permute-done.2, bf16[64,256,128]{2,1,0:T(8,128)(2,1)S(1)} %copy-done.4, bf16[3,2,128,128]{3,2,1,0:T(8,128)(2,1)S(1)} %copy-done.7), kind=kOutput, calls=%fused_computation.3 | convolution fusion | flops 551550976 | bytes 18907140 | tf_op jit(solution)/shard_map/stc,cd->std/dot_general | solution.py:19
  175.5 5.4 %collective-permute-start.3 = (bf16[64,128,128]{2,1,0:T(8,128)(2,1)S(1)}, bf16[64,128,128]{2,1,0:T(8,128)(2,1)S(1)}, u32[]{:S(2)}, u32[]{:S(2)}) collective-permute-start(bf16[64,128,128]{2,1,0:T(8,128)(2,1)S(1)} %slice.130), channel_id=1, source_target_pairs={{0,2},{2,4},{4,6},{6,8},{8,10},{10,12},{12,14},{1,3},{3,5},{5,7},{... | collective-permute-start | bytes 6291464 | tf_op jit(solution)/shard_map/ppermute | solution.py:13
  180.9 4.5 fusion.39
  185.3 37.7 %collective-permute-done.3 = bf16[64,128,128]{2,1,0:T(8,128)(2,1)S(1)} collective-permute-done((bf16[64,128,128]{2,1,0:T(8,128)(2,1)S(1)}, bf16[64,128,128]{2,1,0:T(8,128)(2,1)S(1)}, u32[]{:S(2)}, u32[]{:S(2)}) %collective-permute-start.3) | collective-permute-done | bytes 2097184 | tf_op jit(solution)/shard_map/ppermute | solution.py:13
  223.0 5.9 %add_convert_fusion.1 = bf16[64,256,128]{2,1,0:T(8,128)(2,1)S(1)} fusion(f32[64,256,128]{2,1,0:T(8,128)} %fusion.39, bf16[64,256,128]{2,1,0:T(8,128)(2,1)S(1)} %copy-done.4, s32[]{:T(128)S(6)} %select_n.16, bf16[64,128,128]{2,1,0:T(8,128)(2,1)S(1)} %collective-permute-done.3, bf16[64,256,128]{2,1,0:T(8,128)(2,1)S(1)} %maximum_convert_fusion.1, ...), kind=kOutput, calls=%fused_computation.2 | convolution fusion | flops 555745280 | bytes 23101444 | tf_op jit(solution)/shard_map/stc,cd->std/dot_general | solution.py:19
  231.1 6.8 %collective-permute-start.4 = (bf16[64,128,128]{2,1,0:T(8,128)(2,1)S(1)}, bf16[64,128,128]{2,1,0:T(8,128)(2,1)}, u32[]{:S(2)}, u32[]{:S(2)}) collective-permute-start(bf16[64,128,128]{2,1,0:T(8,128)(2,1)S(1)} %slice.131), channel_id=1, source_target_pairs={{0,2},{2,4},{4,6},{6,8},{8,10},{10,12},{12,14},{1,3},{3,5},{5,7},{... | collective-permute-start | bytes 6291464 | tf_op jit(solution)/shard_map/ppermute | solution.py:13
  239.1 3.6 fusion.36
  242.7 35.2 %collective-permute-done.4 = bf16[64,128,128]{2,1,0:T(8,128)(2,1)} collective-permute-done((bf16[64,128,128]{2,1,0:T(8,128)(2,1)S(1)}, bf16[64,128,128]{2,1,0:T(8,128)(2,1)}, u32[]{:S(2)}, u32[]{:S(2)}) %collective-permute-start.4) | collective-permute-done | bytes 2097184 | tf_op jit(solution)/shard_map/ppermute | solution.py:13
  277.9 4.4 maximum_convert_fusion
  282.5 5.8 %collective-permute-start.5 = (bf16[64,128,128]{2,1,0:T(8,128)(2,1)S(1)}, bf16[64,128,128]{2,1,0:T(8,128)(2,1)S(1)}, u32[]{:S(2)}, u32[]{:S(2)}) collective-permute-start(bf16[64,128,128]{2,1,0:T(8,128)(2,1)S(1)} %slice.132), channel_id=1, source_target_pairs={{0,2},{2,4},{4,6},{6,8},{8,10},{10,12},{12,14},{1,3},{3,5},{5,7},{... | collective-permute-start | bytes 6291464 | tf_op jit(solution)/shard_map/ppermute | solution.py:13
  288.3 40.2 %collective-permute-done.5 = bf16[64,128,128]{2,1,0:T(8,128)(2,1)S(1)} collective-permute-done((bf16[64,128,128]{2,1,0:T(8,128)(2,1)S(1)}, bf16[64,128,128]{2,1,0:T(8,128)(2,1)S(1)}, u32[]{:S(2)}, u32[]{:S(2)}) %collective-permute-start.5) | collective-permute-done | bytes 2097184 | tf_op jit(solution)/shard_map/ppermute | solution.py:13
  328.6 5.5 %fusion.1 = f32[64,256,128]{2,1,0:T(8,128)} fusion(s32[]{:T(128)S(6)} %select_n.17, bf16[64,128,128]{2,1,0:T(8,128)(2,1)S(1)} %collective-permute-done.5, bf16[64,256,128]{2,1,0:T(8,128)(2,1)S(1)} %maximum_convert_fusion, bf16[3,2,128,128]{3,2,1,0:T(8,128)(2,1)S(1)} %copy-done.8), kind=kOutput, calls=%fused_computation.19 | convolution fusion | flops 545259520 | bytes 14712836 | tf_op jit(solution)/shard_map/stc,cd->std/dot_general | solution.py:19
  334.1 8.2 %fusion.18 = f32[1,64,256]{2,0,1:T(1,128)S(1)} fusion(f32[64,256,128]{2,1,0:T(8,128)} %fusion.1, bf16[64,256,128]{2,1,0:T(8,128)(2,1)} %copy-done.1, bf16[64,256,128]{2,1,0:T(8,128)(2,1)} %copy-done.6, bf16[3,2,128,128]{3,2,1,0:T(8,128)(2,1)S(1)} %copy-done.8, bf16[128]{0:T(256)(128)(2,1)S(1)} %copy-done.11), kind=kOutput, calls=%fused_computation.30 | convolution fusion | flops 551550976 | bytes 16876032 | tf_op jit(solution)/shard_map/stc,c->st/dot_general | solution.py:50
  342.6 39.1 %psum.42 = f32[64,64]{1,0:T(8,128)S(1)} all-reduce(f32[64,64]{1,0:T(8,128)S(1)} %fusion.89), channel_id=1, replica_groups=mesh['grp'=2,'tm'=8,'sens'=2] {'tm'}, use_global_device_ids=true, to_apply=%region_0.1 | all-reduce | flops 4096 | bytes 32768 | tf_op jit(solution)/shard_map/psum | solution.py:28
  386.3 5.8 %cholesky.44 = f32[64,64]{1,0:T(8,128)S(1)} custom-call(f32[64,64]{1,0:T(8,128)S(1)} %fusion.58), custom_call_target="Cholesky" | custom-call | tf_op jit(solution)/shard_map/jit(cholesky)/cholesky | solution.py:55
  393.6 4.9 %custom-call.11 = f32[1,64,64]{1,2,0:T(8,128)S(1)} custom-call(f32[1,64,64]{2,1,0:T(8,128)S(1)} %fusion.31), custom_call_target="InvertDiagBlocksLowerTriangular" | custom-call | tf_op jit(solution)/shard_map/jit(_solve_triangular)/triangular_solve | solution.py:36
  398.5 9.6 %all-reduce.3.cloned.1.call-done = f32[64,256]{1,0:T(8,128)} async-done(((f32[64,256]{1,0:T(8,128)}), f32[64,256]{1,0:T(8,128)}) %all-reduce.3.cloned.1.call-update) | async-done | bytes 65552 | tf_op jit(solution)/shard_map/psum | solution.py:32
  409.4 37.4 %psum.45 = f32[64,64]{1,0:T(8,128)S(1)} all-reduce(f32[64,64]{1,0:T(8,128)S(1)} %fusion.92), channel_id=1, replica_groups=mesh['grp'=2,'tm'=8,'sens'=2] {'tm'}, use_global_device_ids=true, to_apply=%region_5.8 | all-reduce | flops 4096 | bytes 32768 | tf_op jit(solution)/shard_map/psum | solution.py:28
  451.4 5.8 %cholesky.55 = f32[64,64]{1,0:T(8,128)S(1)} custom-call(f32[64,64]{1,0:T(8,128)S(1)} %fusion.55), custom_call_target="Cholesky" | custom-call | tf_op jit(solution)/shard_map/jit(cholesky)/cholesky | solution.py:59
  458.8 4.9 %custom-call.9 = f32[1,64,64]{1,2,0:T(8,128)S(1)} custom-call(f32[1,64,64]{2,1,0:T(8,128)S(1)} %fusion.32), custom_call_target="InvertDiagBlocksLowerTriangular" | custom-call | tf_op jit(solution)/shard_map/jit(_solve_triangular)/triangular_solve | solution.py:36
  463.9 14.9 %all-reduce.5.cloned.1.call-done = f32[64,256]{1,0:T(8,128)} async-done(((f32[64,256]{1,0:T(8,128)}), f32[64,256]{1,0:T(8,128)}) %all-reduce.5.cloned.1.call-update) | async-done | bytes 65552 | tf_op jit(solution)/shard_map/psum | solution.py:32
  (58 shorter events, 23.1 us)
Async XLA Ops:
  6.5 335.8 %copy-start = (f32[256,64]{0,1:T(8,128)S(1)}, f32[256,64]{0,1:T(8,128)}, u32[]{:S(2)}) copy-start(f32[256,64]{0,1:T(8,128)} %param.12) | copy-start | bytes 196612
  6.5 8.1 %copy-start.10 = (s32[3]{0:T(128)S(1)}, s32[3]{0:T(128)}, u32[]{:S(2)}) copy-start(s32[3]{0:T(128)} %param.16) | copy-start | bytes 40
  6.5 10.1 %copy-start.7 = (bf16[3,2,128,128]{3,2,1,0:T(8,128)(2,1)S(1)}, bf16[3,2,128,128]{3,2,1,0:T(8,128)(2,1)}, u32[]{:S(2)}) copy-start(bf16[3,2,128,128]{3,2,1,0:T(8,128)(2,1)} %param.13) | copy-start | bytes 589828
  6.5 401.6 %all-reduce.3.cloned.1.call-start = ((), (), s32[]{:S(2)}) async-start(), calls=%async_computation | async-start | bytes 131072 | tf_op jit(solution)/shard_map/psum | solution.py:32
  8.3 49.8 %collective-permute-start = (bf16[64,128,128]{2,1,0:T(8,128)(2,1)S(1)}, bf16[64,128,128]{2,1,0:T(8,128)(2,1)}, u32[]{:S(2)}, u32[]{:S(2)}) collective-permute-start(bf16[64,128,128]{2,1,0:T(8,128)(2,1)S(1)} %slice.107), channel_id=1, source_target_pairs={{0,2},{2,4},{4,6},{6,8},{8,10},{10,12},{12,14},{1,3},{3,5},{5,7},{... | collective-permute-start | bytes 6291464 | tf_op jit(solution)/shard_map/ppermute | solution.py:13
  16.6 41.5 %copy-start.5 = (bf16[64,256,128]{2,1,0:T(8,128)(2,1)S(1)}, bf16[64,256,128]{2,1,0:T(8,128)(2,1)}, u32[]{:S(2)}) copy-start(bf16[64,256,128]{2,1,0:T(8,128)(2,1)} %param.10) | copy-start | bytes 12582916
  64.5 4.9 %copy-start.8 = (bf16[3,2,128,128]{3,2,1,0:T(8,128)(2,1)S(1)}, bf16[3,2,128,128]{3,2,1,0:T(8,128)(2,1)}, u32[]{:S(2)}) copy-start(bf16[3,2,128,128]{3,2,1,0:T(8,128)(2,1)} %param.14) | copy-start | bytes 589828
  64.7 48.5 %collective-permute-start.1 = (bf16[64,128,128]{2,1,0:T(8,128)(2,1)S(1)}, bf16[64,128,128]{2,1,0:T(8,128)(2,1)S(1)}, u32[]{:S(2)}, u32[]{:S(2)}) collective-permute-start(bf16[64,128,128]{2,1,0:T(8,128)(2,1)S(1)} %slice.128), channel_id=1, source_target_pairs={{0,2},{2,4},{4,6},{6,8},{8,10},{10,12},{12,14},{1,3},{3,5},{5,7},{... | collective-permute-start | bytes 6291464 | tf_op jit(solution)/shard_map/ppermute | solution.py:13
  119.1 2.0 copy-start.3
  121.3 47.6 %collective-permute-start.2 = (bf16[64,128,128]{2,1,0:T(8,128)(2,1)S(1)}, bf16[64,128,128]{2,1,0:T(8,128)(2,1)}, u32[]{:S(2)}, u32[]{:S(2)}) collective-permute-start(bf16[64,128,128]{2,1,0:T(8,128)(2,1)S(1)} %slice.129), channel_id=1, source_target_pairs={{0,2},{2,4},{4,6},{6,8},{8,10},{10,12},{12,14},{1,3},{3,5},{5,7},{... | collective-permute-start | bytes 6291464 | tf_op jit(solution)/shard_map/ppermute | solution.py:13
  128.3 40.5 %copy-start.4 = (bf16[64,256,128]{2,1,0:T(8,128)(2,1)S(1)}, bf16[64,256,128]{2,1,0:T(8,128)(2,1)}, u32[]{:S(2)}) copy-start(bf16[64,256,128]{2,1,0:T(8,128)(2,1)} %copy-done.3) | copy-start | bytes 12582916
  175.5 47.6 %collective-permute-start.3 = (bf16[64,128,128]{2,1,0:T(8,128)(2,1)S(1)}, bf16[64,128,128]{2,1,0:T(8,128)(2,1)S(1)}, u32[]{:S(2)}, u32[]{:S(2)}) collective-permute-start(bf16[64,128,128]{2,1,0:T(8,128)(2,1)S(1)} %slice.130), channel_id=1, source_target_pairs={{0,2},{2,4},{4,6},{6,8},{8,10},{10,12},{12,14},{1,3},{3,5},{5,7},{... | collective-permute-start | bytes 6291464 | tf_op jit(solution)/shard_map/ppermute | solution.py:13
  229.0 2.0 copy-start.1
  231.1 46.8 %collective-permute-start.4 = (bf16[64,128,128]{2,1,0:T(8,128)(2,1)S(1)}, bf16[64,128,128]{2,1,0:T(8,128)(2,1)}, u32[]{:S(2)}, u32[]{:S(2)}) collective-permute-start(bf16[64,128,128]{2,1,0:T(8,128)(2,1)S(1)} %slice.131), channel_id=1, source_target_pairs={{0,2},{2,4},{4,6},{6,8},{8,10},{10,12},{12,14},{1,3},{3,5},{5,7},{... | collective-permute-start | bytes 6291464 | tf_op jit(solution)/shard_map/ppermute | solution.py:13
  239.1 38.8 %copy-start.2 = (bf16[64,256,128]{2,1,0:T(8,128)(2,1)S(1)}, bf16[64,256,128]{2,1,0:T(8,128)(2,1)}, u32[]{:S(2)}) copy-start(bf16[64,256,128]{2,1,0:T(8,128)(2,1)} %copy-done.1) | copy-start | bytes 12582916
  282.4 46.2 %copy-start.6 = (bf16[64,256,128]{2,1,0:T(8,128)(2,1)}, bf16[64,256,128]{2,1,0:T(8,128)(2,1)S(1)}, u32[]{:S(2)}) copy-start(bf16[64,256,128]{2,1,0:T(8,128)(2,1)S(1)} %maximum_convert_fusion) | copy-start | bytes 12582916
  282.5 51.5 %copy-start.11 = (bf16[128]{0:T(256)(128)(2,1)S(1)}, bf16[128]{0:T(256)(128)(2,1)}, u32[]{:S(2)}) copy-start(bf16[128]{0:T(256)(128)(2,1)} %param.15) | copy-start | bytes 772
  282.5 46.0 %collective-permute-start.5 = (bf16[64,128,128]{2,1,0:T(8,128)(2,1)S(1)}, bf16[64,128,128]{2,1,0:T(8,128)(2,1)S(1)}, u32[]{:S(2)}, u32[]{:S(2)}) collective-permute-start(bf16[64,128,128]{2,1,0:T(8,128)(2,1)S(1)} %slice.132), channel_id=1, source_target_pairs={{0,2},{2,4},{4,6},{6,8},{8,10},{10,12},{12,14},{1,3},{3,5},{5,7},{... | collective-permute-start | bytes 6291464 | tf_op jit(solution)/shard_map/ppermute | solution.py:13
  334.1 8.2 %copy-start.9 = (f32[64,256]{1,0:T(8,128)S(1)}, f32[64,256]{1,0:T(8,128)}, u32[]{:S(2)}) copy-start(f32[64,256]{1,0:T(8,128)} %param.11) | copy-start | bytes 196612
  392.9 85.9 %all-reduce.5.cloned.1.call-start = ((), (), s32[]{:S(2)}) async-start(), calls=%async_computation.1 | async-start | bytes 131072 | tf_op jit(solution)/shard_map/psum | solution.py:32
Sparse Core Ops, SparseCore 0:
  393.0 15.0 all-reduce.2
  463.8 14.9 all-reduce.4
where the time goes:
time: 488 us
  waiting for transfers between devices  245 us (50%)
  blocking collectives  83.3 us (17%)
  matrix products  74.8 us (15%)
  starting transfers between devices  34.6 us (7%)
  other arithmetic  24.3 us (5%)
  between operations  17.7 us (4%)
  local copies, waits for them, and re-layouts  7.45 us (2%)
    ppermute x6, waiting for transfers between devices, shifted(): return lax.ppermute(value, axis, pairs)  221 us
    psum x2, blocking collectives, time_total(): return lax.psum(value, 'tm')  76.5 us
    ppermute x6, starting transfers between devices, shifted(): return lax.ppermute(value, axis, pairs)  34.6 us
    dot_general x6, matrix products, dilated(): jnp.einsum('stc,cd->std', moved, weight[0], preferred_element_type=jnp.fl...  34.5 us
    dot_general x5, matrix products, dilated(): jnp.einsum('stc,cd->std', current, weight[1], preferred_element_type=jnp....  26.1 us
    psum x2, waiting for transfers between devices, joint_total(): lax.psum((cross, jnp.dot(sketch.T, sketch, precision=lax.Precision.HIGHES...  24.5 us
    another operation x4, other arithmetic, lower_solve(): return jax.scipy.linalg.solve_triangular(factor, value, lower=True)  11.1 us
  transfers between devices with their start and end apart: 8, of which 8 were waited for; matrix products, arithmetic and copies ran while one was open for 7% of the time, Pallas kernels for 0%

commit v1 on v0

--- a/solution.py
+++ b/solution.py
@@ -1,10 +1,15 @@
+import functools
+
 import jax
 import jax.numpy as jnp
 from jax import lax
+from jax.experimental import pallas as pl
+from jax.experimental.pallas import tpu as pltpu
 from jax.sharding import PartitionSpec as P
 
-LAYERS = 3
 DMAX = 128
+MESH = pl.DeviceIdType.MESH
+HIGH = lax.Precision.HIGHEST
 
 
 def shifted(value, axis, by):
@@ -29,18 +34,18 @@
 
 
 def joint_total(cross, sketch):
-    return lax.psum((cross, jnp.dot(sketch.T, sketch, precision=lax.Precision.HIGHEST)), "sens")
+    return lax.psum((cross, jnp.dot(sketch.T, sketch, precision=HIGH)), "sens")
 
 
 def lower_solve(factor, value):
     return jax.scipy.linalg.solve_triangular(factor, value, lower=True)
 
 
-def on_device(
+def halo_form(
     features, target, test_matrix, leading_conv_taps, trailing_conv_taps, readout, dilations
 ):
     hidden = features
-    for layer in range(LAYERS):
+    for layer in range(leading_conv_taps.shape[0]):
         dist = dilations[layer]
         inner = jax.nn.relu(
             dilated(causal_tail(hidden), hidden, dist, leading_conv_taps[layer])
@@ -49,17 +54,298 @@
         hidden = (hidden.astype(jnp.float32) + branch).astype(jnp.bfloat16)
     prediction_values = jnp.einsum("stc,c->st", hidden, readout, preferred_element_type=jnp.float32)
     resid = target - prediction_values
-    high = lax.Precision.HIGHEST
-    sketch = time_total(jnp.dot(resid, test_matrix, precision=high))
-    cross, gram = joint_total(jnp.dot(resid.T, sketch, precision=high), sketch)
+    sketch = time_total(jnp.dot(resid, test_matrix, precision=HIGH))
+    cross, gram = joint_total(jnp.dot(resid.T, sketch, precision=HIGH), sketch)
     factor = jnp.linalg.cholesky(gram)
     projected = lower_solve(factor, cross.T).T
-    sketch_two = time_total(jnp.dot(resid, projected, precision=high))
-    cross_two, gram_two = joint_total(jnp.dot(sketch_two.T, resid, precision=high), sketch_two)
+    sketch_two = time_total(jnp.dot(resid, projected, precision=HIGH))
+    cross_two, gram_two = joint_total(jnp.dot(sketch_two.T, resid, precision=HIGH), sketch_two)
     factor_two = jnp.linalg.cholesky(gram_two)
     coef = lower_solve(factor_two, cross_two)
     basis_two = lower_solve(factor_two, sketch_two.T).T
-    return resid - jnp.dot(basis_two, coef, precision=high)
+    return resid - jnp.dot(basis_two, coef, precision=HIGH)
+
+
+def exchange_kernel(
+    peers, sides, chunk, rank,
+    dil_ref, x_ref, tgt_ref, test_ref, lead_ref, trail_ref, read_ref,
+    resid_ref, total_ref,
+    recv, taps, pred, pred_in, tgt_in, part, part_in, red,
+    own_sem, send_sem, recv_sem, tgt_send, tgt_recv, p_own, p_send, p_recv,
+    s_own, s_send, s_recv, g_own, g_send, g_recv,
+):
+    me = lax.axis_index("tm")
+    side = lax.axis_index("sens")
+    other_side = 1 - side
+    per = x_ref.shape[0] // peers
+    steps = x_ref.shape[1]
+    channels = x_ref.shape[2]
+    chunks = per // chunk
+    layers = lead_ref.shape[0]
+
+    barrier = pltpu.get_barrier_semaphore()
+    for k in range(1, peers):
+        for s in range(sides):
+            pl.semaphore_signal(barrier, inc=1, device_id={"tm": lax.rem(me + k, peers), "sens": lax.rem(side + s, sides)}, device_id_type=MESH)
+    pl.semaphore_signal(barrier, inc=1, device_id={"sens": other_side}, device_id_type=MESH)
+    pl.semaphore_wait(barrier, peers * sides - 1)
+
+    def feature_copy(c, k):
+        to = lax.rem(me + k, peers)
+        return pltpu.make_async_remote_copy(
+            src_ref=x_ref.at[pl.ds(to * per + c * chunk, chunk)],
+            dst_ref=recv.at[c, me],
+            send_sem=send_sem.at[c, k],
+            recv_sem=recv_sem.at[c, me],
+            device_id={"tm": to},
+            device_id_type=MESH,
+        )
+
+    def feature_arrival(c, src):
+        return pltpu.make_async_remote_copy(
+            src_ref=x_ref.at[pl.ds(0, chunk)],
+            dst_ref=recv.at[c, src],
+            send_sem=send_sem.at[c, 1],
+            recv_sem=recv_sem.at[c, src],
+            device_id={"tm": lax.rem(me + 1, peers)},
+            device_id_type=MESH,
+        )
+
+    def own_copy(c):
+        return pltpu.make_async_copy(
+            x_ref.at[pl.ds(me * per + c * chunk, chunk)], recv.at[c, me], recv_sem.at[c, me]
+        )
+
+    order = [peers // 2]
+    for k in range(1, peers // 2):
+        order += [peers // 2 - k, peers // 2 + k]
+    for c in range(chunks):
+        for k in order:
+            feature_copy(c, k).start()
+        own_copy(c).start()
+    tgt_copy = pltpu.make_async_remote_copy(
+        src_ref=tgt_ref, dst_ref=tgt_in, send_sem=tgt_send, recv_sem=tgt_recv,
+        device_id={"sens": other_side}, device_id_type=MESH,
+    )
+    tgt_copy.start()
+
+    for i in range(2 * layers):
+        for s in range(chunk):
+            taps[i, s, 0:DMAX, :] = jnp.zeros((DMAX, channels), jnp.float32)
+
+    def conv(value, weight, i, j, dist):
+        both = jnp.dot(value, weight, preferred_element_type=jnp.float32)
+        start = DMAX + j * steps
+        outs = []
+        for s in range(chunk):
+            taps[i, s, pl.ds(pl.multiple_of(start, DMAX), steps), :] = both[s * steps:(s + 1) * steps, :channels]
+        for s in range(chunk):
+            outs.append(taps[i, s, pl.ds(start - dist, steps), :])
+        return jnp.concatenate(outs, axis=0) + both[:, channels:]
+
+    def step(index, carry):
+        c = index // peers
+        j = index % peers
+        feature_arrival(c, j).wait_recv()
+        hidden = recv[c, j].reshape(chunk * steps, channels)
+        for layer in range(layers):
+            dist = dil_ref[layer]
+            inner = jnp.maximum(conv(hidden, lead_ref[layer], 2 * layer, j, dist), 0.0).astype(jnp.bfloat16)
+            branch = jnp.maximum(conv(inner, trail_ref[layer], 2 * layer + 1, j, dist), 0.0)
+            hidden = (hidden.astype(jnp.float32) + branch).astype(jnp.bfloat16)
+        for s in range(chunk):
+            row = lax.dot_general(
+                read_ref[...], hidden[s * steps:(s + 1) * steps], (((1,), (1,)), ((), ())),
+                preferred_element_type=jnp.float32,
+            )
+            pred[j, pl.ds(c * chunk + s, 1), :] = row[0:1, :]
+        return carry
+
+    lax.fori_loop(0, chunks * peers, step, 0)
+
+    def pred_copy(k, s):
+        to = lax.rem(me + k, peers)
+        return pltpu.make_async_remote_copy(
+            src_ref=pred.at[to],
+            dst_ref=pred_in.at[side * peers + me],
+            send_sem=p_send.at[s, k],
+            recv_sem=p_recv.at[side * peers + me],
+            device_id={"tm": to, "sens": lax.rem(side + s, sides)},
+            device_id_type=MESH,
+        )
+
+    everyone = [(k, s) for k in range(peers) for s in range(sides) if (k, s) != (0, 0)]
+    for k, s in everyone:
+        pred_copy(k, s).start()
+    own_pred = pltpu.make_async_copy(pred.at[me], pred_in.at[side * peers + me], p_recv.at[side * peers + me])
+    own_pred.start()
+    tgt_copy.wait()
+    for n in range(peers * sides):
+        pltpu.make_async_remote_copy(
+            src_ref=pred.at[0], dst_ref=pred_in.at[n], send_sem=p_send.at[0, 1], recv_sem=p_recv.at[n],
+            device_id={"sens": other_side}, device_id_type=MESH,
+        ).wait_recv()
+    half = peers * per
+    first = side == 0
+    own_target = tgt_ref[...]
+    far_target = tgt_in[...]
+    low = jnp.where(first, own_target, far_target)
+    high = jnp.where(first, far_target, own_target)
+    everything = pred_in[...].reshape(sides * half, steps)
+    resid = jnp.concatenate([low, high], axis=0) - everything
+    resid_ref[...] = resid
+    gram = lax.dot_general(resid, resid, (((1,), (1,)), ((), ())), precision=HIGH, preferred_element_type=jnp.float32)
+    sketch = jnp.dot(resid, test_ref[...], precision=HIGH, preferred_element_type=jnp.float32)
+    rows = part.shape[1]
+    part[:, :, 0:sides * half] = gram.reshape(peers, rows, sides * half)
+    part[:, :, sides * half:] = sketch.reshape(peers, rows, test_ref.shape[1])
+
+    def sum_copy(k):
+        to = lax.rem(me + k, peers)
+        return pltpu.make_async_remote_copy(
+            src_ref=part.at[to], dst_ref=part_in.at[me], send_sem=s_send.at[k], recv_sem=s_recv.at[me],
+            device_id={"tm": to}, device_id_type=MESH,
+        )
+
+    def share_copy(k):
+        to = lax.rem(me + k, peers)
+        return pltpu.make_async_remote_copy(
+            src_ref=red, dst_ref=total_ref.at[me], send_sem=g_send.at[k], recv_sem=g_recv.at[me],
+            device_id={"tm": to}, device_id_type=MESH,
+        )
+
+    for k in range(1, peers):
+        sum_copy(k).start()
+    own_part = pltpu.make_async_copy(part.at[me], part_in.at[me], s_recv.at[me])
+    own_part.start()
+    acc = None
+    for n in range(peers):
+        pltpu.make_async_remote_copy(
+            src_ref=part.at[0], dst_ref=part_in.at[n], send_sem=s_send.at[1], recv_sem=s_recv.at[n],
+            device_id={"tm": lax.rem(me + 1, peers)}, device_id_type=MESH,
+        ).wait_recv()
+        acc = part_in[n] if acc is None else acc + part_in[n]
+    red[...] = acc
+    for k in range(1, peers):
+        share_copy(k).start()
+    own_red = pltpu.make_async_copy(red, total_ref.at[me], g_recv.at[me])
+    own_red.start()
+    for n in range(peers):
+        pltpu.make_async_remote_copy(
+            src_ref=red, dst_ref=total_ref.at[n], send_sem=g_send.at[1], recv_sem=g_recv.at[n],
+            device_id={"tm": lax.rem(me + 1, peers)}, device_id_type=MESH,
+        ).wait_recv()
+    for k in range(1, peers):
+        for c in range(chunks):
+            feature_copy(c, k).wait_send()
+        sum_copy(k).wait_send()
+        share_copy(k).wait_send()
+    for k, s in everyone:
+        pred_copy(k, s).wait_send()
+
+
+def orthonormal(sketch):
+    rank = sketch.shape[1]
+    gram = lax.dot_general(sketch, sketch, (((0,), (0,)), ((), ())), precision=HIGH, preferred_element_type=jnp.float32)
+    row_of = lax.broadcasted_iota(jnp.int32, (rank, rank), 0)
+    col_of = lax.broadcasted_iota(jnp.int32, (rank, rank), 1)
+    eye = jnp.where(row_of == col_of, 1.0, 0.0).astype(jnp.float32)
+    both = jnp.concatenate([gram, eye], axis=1)
+    blocks = [both[8 * b:8 * b + 8] for b in range(rank // 8)]
+    sub = lax.broadcasted_iota(jnp.int32, (8, 1), 0)
+    for k in range(rank):
+        top = k // 8
+        pivot_row = blocks[top][k % 8:k % 8 + 1, :]
+        inverse = 1.0 / pivot_row[:, k:k + 1]
+        scaled = pivot_row * inverse
+        for b in range(top, rank // 8):
+            col = blocks[b][:, k:k + 1]
+            if b == top:
+                col = jnp.where(sub > k % 8, col, 0.0)
+            blocks[b] = blocks[b] - col * scaled
+    both = jnp.concatenate(blocks, axis=0)
+    pivots = jnp.sum(jnp.where(row_of == col_of, both[:, :rank], 0.0), axis=1, keepdims=True)
+    inverse_factor = both[:, rank:] * (1.0 / jnp.sqrt(pivots))
+    return lax.dot_general(sketch, inverse_factor, (((1,), (1,)), ((), ())), precision=HIGH, preferred_element_type=jnp.float32)
+
+
+def finish_kernel(own, resid_ref, total_ref, out_ref, basis_ref):
+    side = lax.axis_index("sens")
+    total = total_ref[...].reshape(resid_ref.shape[0], total_ref.shape[2])
+    size = resid_ref.shape[0]
+    gram = total[:, :size]
+    basis = orthonormal(total[:, size:])
+    sketch = jnp.dot(gram, basis, precision=HIGH, preferred_element_type=jnp.float32)
+    basis = orthonormal(sketch)
+    basis_ref[...] = basis
+    resid = resid_ref[...]
+    coef = lax.dot_general(basis, resid, (((0,), (0,)), ((), ())), precision=HIGH, preferred_element_type=jnp.float32)
+    mine = pl.ds(pl.multiple_of(side * own, own), own)
+    out_ref[...] = resid_ref[mine, :] - jnp.dot(basis_ref[mine, :], coef, precision=HIGH, preferred_element_type=jnp.float32)
+
+
+def sensor_form(
+    features, target, test_matrix, leading_conv_taps, trailing_conv_taps, readout, dilations
+):
+    peers = lax.axis_size("tm")
+    sides = lax.axis_size("sens")
+    own, steps, channels = features.shape
+    rank = test_matrix.shape[1]
+    layers = leading_conv_taps.shape[0]
+    per = own // peers
+    chunk = 2 if per % 2 == 0 else 1
+    chunks = per // chunk
+    size = own * sides
+    lead = jnp.concatenate([leading_conv_taps[:, 0], leading_conv_taps[:, 1]], axis=-1)
+    trail = jnp.concatenate([trailing_conv_taps[:, 0], trailing_conv_taps[:, 1]], axis=-1)
+    read = jnp.broadcast_to(readout[None, :], (16, channels))
+    vmem = pl.BlockSpec(memory_space=pltpu.VMEM)
+    dma = pltpu.SemaphoreType.DMA
+    resid, total = pl.pallas_call(
+        functools.partial(exchange_kernel, peers, sides, chunk, rank),
+        out_shape=(
+            jax.ShapeDtypeStruct((size, steps), jnp.float32),
+            jax.ShapeDtypeStruct((peers, size // peers, size + rank), jnp.float32),
+        ),
+        in_specs=[
+            pl.BlockSpec(memory_space=pltpu.SMEM), pl.BlockSpec(memory_space=pl.ANY),
+            vmem, vmem, vmem, vmem, vmem,
+        ],
+        out_specs=(vmem, vmem),
+        scratch_shapes=[
+            pltpu.VMEM((chunks, peers, chunk, steps, channels), jnp.bfloat16),
+            pltpu.VMEM((2 * layers, chunk, DMAX + peers * steps, channels), jnp.float32),
+            pltpu.VMEM((peers, per, steps), jnp.float32),
+            pltpu.VMEM((peers * sides, per, steps), jnp.float32),
+            pltpu.VMEM((own, steps), jnp.float32),
+            pltpu.VMEM((peers, size // peers, size + rank), jnp.float32),
+            pltpu.VMEM((peers, size // peers, size + rank), jnp.float32),
+            pltpu.VMEM((size // peers, size + rank), jnp.float32),
+            dma, dma((chunks, peers)), dma((chunks, peers)), dma, dma,
+            dma, dma((sides, peers)), dma((peers * sides,)),
+            dma, dma((peers,)), dma((peers,)),
+            dma, dma((peers,)), dma((peers,)),
+        ],
+        compiler_params=pltpu.CompilerParams(
+            collective_id=0, has_side_effects=True, vmem_limit_bytes=56 * 1024 * 1024
+        ),
+        name="exchange",
+    )(dilations, features, target, test_matrix, lead, trail, read)
+    return pl.pallas_call(
+        functools.partial(finish_kernel, own),
+        out_shape=jax.ShapeDtypeStruct((own, steps), jnp.float32),
+        in_specs=[vmem, vmem],
+        out_specs=vmem,
+        scratch_shapes=[pltpu.VMEM((size, rank), jnp.float32)],
+        name="finish",
+    )(resid, total)
+
+
+def on_device(features, *rest):
+    peers = lax.axis_size("tm")
+    if lax.axis_size("sens") == 2 and features.shape[0] % (8 * peers) == 0:
+        return sensor_form(features, *rest)
+    return halo_form(features, *rest)
 
 
 def solution(mesh):

time: 488 us -> 153 us (0.31)
  waiting for transfers between devices: 245 us -> 0 us
  Pallas kernels: 0 us -> 147 us
  blocking collectives: 83.3 us -> 0 us
  matrix products: 74.8 us -> 0 us
  starting transfers between devices: 34.6 us -> 0 us
  other arithmetic: 24.3 us -> 0.8 us
  between operations: 17.7 us -> 0.02 us
    ppermute x6 -> x0, waiting for transfers between devices: 221 us -> none  [shifted(): return lax.ppermute(value, axis, pairs)]
    pallas_call x0 -> x2, Pallas kernels: none -> 147 us  [the longest x1 133 us: sensor_form(): pl.pallas_call(functools.partial(exchange_kernel, peers, sides, chunk, ra...]
    psum x4 -> x0, blocking collectives: 83.3 us -> none  [the longest x2 76.5 us: time_total(): return lax.psum(value, 'tm')]
    dot_general x19 -> x0, matrix products: 72.4 us -> none  [the longest x6 34.5 us: dilated(): jnp.einsum('stc,cd->std', moved, weight[0], preferred_element_type=jnp.fl...]
    ppermute x6 -> x0, starting transfers between devices: 34.6 us -> none  [shifted(): return lax.ppermute(value, axis, pairs)]
    psum x2 -> x0, waiting for transfers between devices: 24.5 us -> none  [joint_total(): lax.psum((cross, jnp.dot(sketch.T, sketch, precision=lax.Precision.HIGHES...]
    another operation x10 -> x0, other arithmetic: 24.3 us -> none  [the longest x4 11.1 us: lower_solve(): return jax.scipy.linalg.solve_triangular(factor, value, lower=True)]
  transfers between devices with their start and end apart: 8 -> 0, of which waited for: 8 -> 0; matrix products, arithmetic and copies ran while one was open for 7% -> 0% of each run, Pallas kernels for 0% -> 0%
where the time goes in v1:
time: 153 us; the launch traced here: 152 us
  Pallas kernels  147 us (96%)
  local copies, waits for them, and re-layouts  4.75 us (3%)
    pallas_call x1, Pallas kernels, sensor_form(): pl.pallas_call(functools.partial(exchange_kernel, peers, sides, chunk, ra...  133 us
    pallas_call x1, Pallas kernels, sensor_form(): pl.pallas_call(functools.partial(finish_kernel, own), out_shape=jax.Shape...  14.2 us

profile of v1, /device:TPU:0, one launch (start us, length us, event | category | flops | bytes accessed | tf_op | source)
XLA Modules:
  0.0 152.4 jit_solution(13193060653501597923)
XLA Ops:
  0.0 1.0 slice_bitcast_fusion.1
  1.0 1.0 slice_bitcast_fusion.3
  1.9 0.8 pad_maximum_fusion
  2.7 1.6 %copy.12.test_ref = f32[256,64]{1,0:T(8,128)} copy(f32[256,64]{0,1:T(8,128)} %param.9) | data formatting | bytes 131072 | tf_op args[2]
  4.3 1.2 broadcast_in_dim.2.read_ref
  5.6 132.7 %exchange.1 = (f32[128,256]{1,0:T(8,128)}, f32[8,16,192]{2,1,0:T(8,128)}) custom-call(s32[3]{0:T(128)} %dil_ref.1, bf16[64,256,128]{2,1,0:T(8,128)(2,1)} %x_ref.1, f32[64,256]{1,0:T(8,128)} %tgt_ref.1, f32[256,64]{1,0:T(8,128)} %copy.12.test_ref, bf16[3,128,256]{2,1,0:T(8,128)(2,1)} %get-tuple-element.13.lead_ref, ...), custom_call_target="tpu_custom_call" | custom-call | tf_op jit(solution)/shard_map/exchange/pallas_call | solution.py:304
  138.2 14.2 %finish.1 = f32[64,256]{1,0:T(8,128)} custom-call(f32[128,256]{1,0:T(8,128)} %get-tuple-element.7.resid_ref, f32[8,16,192]{2,1,0:T(8,128)} %get-tuple-element.8.total_ref), custom_call_target="tpu_custom_call" | custom-call | tf_op jit(solution)/shard_map/finish/pallas_call | solution.py:334

commit v2 on v1

--- a/solution.py
+++ b/solution.py
@@ -133,15 +133,18 @@
         for s in range(chunk):
             taps[i, s, 0:DMAX, :] = jnp.zeros((DMAX, channels), jnp.float32)
 
+    read = jnp.broadcast_to(read_ref[...], (16, channels))
+
     def conv(value, weight, i, j, dist):
-        both = jnp.dot(value, weight, preferred_element_type=jnp.float32)
         start = DMAX + j * steps
+        wide = value.astype(jnp.float32)
         outs = []
         for s in range(chunk):
-            taps[i, s, pl.ds(pl.multiple_of(start, DMAX), steps), :] = both[s * steps:(s + 1) * steps, :channels]
+            taps[i, s, pl.ds(pl.multiple_of(start, DMAX), steps), :] = wide[s * steps:(s + 1) * steps]
         for s in range(chunk):
-            outs.append(taps[i, s, pl.ds(start - dist, steps), :])
-        return jnp.concatenate(outs, axis=0) + both[:, channels:]
+            outs.append(taps[i, s, pl.ds(start - dist, steps), :].astype(jnp.bfloat16))
+        joined = jnp.concatenate([jnp.concatenate(outs, axis=0), value], axis=1)
+        return jnp.dot(joined, weight, preferred_element_type=jnp.float32)
 
     def step(index, carry):
         c = index // peers
@@ -155,7 +158,7 @@
             hidden = (hidden.astype(jnp.float32) + branch).astype(jnp.bfloat16)
         for s in range(chunk):
             row = lax.dot_general(
-                read_ref[...], hidden[s * steps:(s + 1) * steps], (((1,), (1,)), ((), ())),
+                read, hidden[s * steps:(s + 1) * steps], (((1,), (1,)), ((), ())),
                 preferred_element_type=jnp.float32,
             )
             pred[j, pl.ds(c * chunk + s, 1), :] = row[0:1, :]
@@ -195,10 +198,10 @@
     resid = jnp.concatenate([low, high], axis=0) - everything
     resid_ref[...] = resid
     gram = lax.dot_general(resid, resid, (((1,), (1,)), ((), ())), precision=HIGH, preferred_element_type=jnp.float32)
-    sketch = jnp.dot(resid, test_ref[...], precision=HIGH, preferred_element_type=jnp.float32)
+    sketch = lax.dot_general(resid, test_ref[...], (((1,), (1,)), ((), ())), precision=HIGH, preferred_element_type=jnp.float32)
     rows = part.shape[1]
     part[:, :, 0:sides * half] = gram.reshape(peers, rows, sides * half)
-    part[:, :, sides * half:] = sketch.reshape(peers, rows, test_ref.shape[1])
+    part[:, :, sides * half:] = sketch.reshape(peers, rows, rank)
 
     def sum_copy(k):
         to = lax.rem(me + k, peers)
@@ -296,9 +299,9 @@
     chunk = 2 if per % 2 == 0 else 1
     chunks = per // chunk
     size = own * sides
-    lead = jnp.concatenate([leading_conv_taps[:, 0], leading_conv_taps[:, 1]], axis=-1)
-    trail = jnp.concatenate([trailing_conv_taps[:, 0], trailing_conv_taps[:, 1]], axis=-1)
-    read = jnp.broadcast_to(readout[None, :], (16, channels))
+    lead = leading_conv_taps.reshape(layers, 2 * channels, channels)
+    trail = trailing_conv_taps.reshape(layers, 2 * channels, channels)
+    read = readout.reshape(1, channels)
     vmem = pl.BlockSpec(memory_space=pltpu.VMEM)
     dma = pltpu.SemaphoreType.DMA
     resid, total = pl.pallas_call(
@@ -330,7 +333,7 @@
             collective_id=0, has_side_effects=True, vmem_limit_bytes=56 * 1024 * 1024
         ),
         name="exchange",
-    )(dilations, features, target, test_matrix, lead, trail, read)
+    )(dilations, features, target, test_matrix.T, lead, trail, read)
     return pl.pallas_call(
         functools.partial(finish_kernel, own),
         out_shape=jax.ShapeDtypeStruct((own, steps), jnp.float32),

time: 153 us -> 142 us (0.928)
  Pallas kernels: 147 us -> 142 us
  local copies, waits for them, and re-layouts: 4.75 us -> 0 us
    pallas_call x1, Pallas kernels: 133 us -> 127 us  [sensor_form(): pl.pallas_call(functools.partial(exchange_kernel, peers, sides, chunk, ra...]
    squeeze x2 -> x0, local copies, waits for them, and re-layouts: 1.92 us -> none  [the longest x1 0.96 us: sensor_form(): leading_conv_taps[:, 0]]
    unnamed x1 -> x0, local copies, waits for them, and re-layouts: 1.59 us -> none
where the time goes in v2:
time: 142 us
  Pallas kernels  142 us (100%)
    pallas_call x1, Pallas kernels, sensor_form(): pl.pallas_call(functools.partial(exchange_kernel, peers, sides, chunk, ra...  127 us
    pallas_call x1, Pallas kernels, sensor_form(): pl.pallas_call(functools.partial(finish_kernel, own), out_shape=jax.Shape...  14.2 us

profile of v2, /device:TPU:0, one launch (start us, length us, event | category | flops | bytes accessed | tf_op | source)
XLA Modules:
  0.0 141.6 jit_solution(6518664397241470609)
XLA Ops:
  0.0 127.4 %exchange.1 = (f32[128,256]{1,0:T(8,128)}, f32[8,16,192]{2,1,0:T(8,128)}) custom-call(s32[3]{0:T(128)} %dil_ref.1, bf16[64,256,128]{2,1,0:T(8,128)(2,1)} %x_ref.1, f32[64,256]{1,0:T(8,128)} %tgt_ref.1, f32[64,256]{1,0:T(8,128)} %bitcast.6, bf16[3,256,128]{2,1,0:T(8,128)(2,1)} %bitcast.4, bf16[3,256,128]{2,1,0:T(8,128)(2,1)} %bitcast.5, bf16[1,128]{1,0:T(2,128)(2,1)} %bitcast.7), custom_call_target="tpu_custom_call" | custom-call | tf_op jit(solution)/shard_map/exchange/pallas_call | solution.py:307
  127.4 14.2 %finish.1 = f32[64,256]{1,0:T(8,128)} custom-call(f32[128,256]{1,0:T(8,128)} %get-tuple-element.7.resid_ref, f32[8,16,192]{2,1,0:T(8,128)} %get-tuple-element.8.total_ref), custom_call_target="tpu_custom_call" | custom-call | tf_op jit(solution)/shard_map/finish/pallas_call | solution.py:337

commit v3 on v2

--- a/solution.py
+++ b/solution.py
@@ -255,17 +255,28 @@
     eye = jnp.where(row_of == col_of, 1.0, 0.0).astype(jnp.float32)
     both = jnp.concatenate([gram, eye], axis=1)
     blocks = [both[8 * b:8 * b + 8] for b in range(rank // 8)]
-    sub = lax.broadcasted_iota(jnp.int32, (8, 1), 0)
-    for k in range(rank):
-        top = k // 8
-        pivot_row = blocks[top][k % 8:k % 8 + 1, :]
-        inverse = 1.0 / pivot_row[:, k:k + 1]
-        scaled = pivot_row * inverse
+    sub = lax.broadcasted_iota(jnp.int32, (8, 2 * rank), 0)
+
+    def spread(block, k):
+        return jnp.broadcast_to(block[:, k:k + 1], block.shape)
+
+    for k in range(0, rank, 2):
+        top, at = k // 8, k % 8
+        row, after = blocks[top][at:at + 1, :], blocks[top][at + 1:at + 2, :]
+        inverse = 1.0 / spread(row, k)
+        cross = spread(row, k + 1)
+        lower = spread(after, k) * inverse
+        upper = cross * inverse
+        inverse_after = 1.0 / (spread(after, k + 1) - lower * cross)
+        scaled = row * inverse
+        scaled_after = (after - lower * row) * inverse_after
         for b in range(top, rank // 8):
-            col = blocks[b][:, k:k + 1]
+            col = spread(blocks[b], k)
+            col_after = spread(blocks[b], k + 1) - col * upper
             if b == top:
-                col = jnp.where(sub > k % 8, col, 0.0)
-            blocks[b] = blocks[b] - col * scaled
+                col = jnp.where(sub > at, col, 0.0)
+                col_after = jnp.where(sub > at + 1, col_after, 0.0)
+            blocks[b] = blocks[b] - col * scaled - col_after * scaled_after
     both = jnp.concatenate(blocks, axis=0)
     pivots = jnp.sum(jnp.where(row_of == col_of, both[:, :rank], 0.0), axis=1, keepdims=True)
     inverse_factor = both[:, rank:] * (1.0 / jnp.sqrt(pivots))

time: 142 us -> 137 us (0.965)
  Pallas kernels: 142 us -> 137 us
    pallas_call x1, Pallas kernels: 14.2 us -> 9.84 us  [sensor_form(): pl.pallas_call(functools.partial(finish_kernel, own), out_shape=jax.Shape...]
where the time goes in v3:
time: 137 us
  Pallas kernels  137 us (100%)
    pallas_call x1, Pallas kernels, sensor_form(): pl.pallas_call(functools.partial(exchange_kernel, peers, sides, chunk, ra...  127 us
    pallas_call x1, Pallas kernels, sensor_form(): pl.pallas_call(functools.partial(finish_kernel, own), out_shape=jax.Shape...  9.84 us

profile of v3, /device:TPU:0, one launch (start us, length us, event | category | flops | bytes accessed | tf_op | source)
XLA Modules:
  0.0 137.2 jit_solution(8283429153285847666)
XLA Ops:
  0.0 127.4 %exchange.1 = (f32[128,256]{1,0:T(8,128)}, f32[8,16,192]{2,1,0:T(8,128)}) custom-call(s32[3]{0:T(128)} %dil_ref.1, bf16[64,256,128]{2,1,0:T(8,128)(2,1)} %x_ref.1, f32[64,256]{1,0:T(8,128)} %tgt_ref.1, f32[64,256]{1,0:T(8,128)} %bitcast.6, bf16[3,256,128]{2,1,0:T(8,128)(2,1)} %bitcast.4, bf16[3,256,128]{2,1,0:T(8,128)(2,1)} %bitcast.5, bf16[1,128]{1,0:T(2,128)(2,1)} %bitcast.7), custom_call_target="tpu_custom_call" | custom-call | tf_op jit(solution)/shard_map/exchange/pallas_call | solution.py:318
  127.4 9.8 %finish.1 = f32[64,256]{1,0:T(8,128)} custom-call(f32[128,256]{1,0:T(8,128)} %get-tuple-element.7.resid_ref, f32[8,16,192]{2,1,0:T(8,128)} %get-tuple-element.8.total_ref), custom_call_target="tpu_custom_call" | custom-call | tf_op jit(solution)/shard_map/finish/pallas_call | solution.py:348

commit v4 on v3

--- a/solution.py
+++ b/solution.py
@@ -70,7 +70,7 @@
     peers, sides, chunk, rank,
     dil_ref, x_ref, tgt_ref, test_ref, lead_ref, trail_ref, read_ref,
     resid_ref, total_ref,
-    recv, taps, pred, pred_in, tgt_in, part, part_in, red,
+    recv, taps, last, pred, pred_in, tgt_in, part, part_in, red,
     own_sem, send_sem, recv_sem, tgt_send, tgt_recv, p_own, p_send, p_recv,
     s_own, s_send, s_recv, g_own, g_send, g_recv,
 ):
@@ -146,25 +146,33 @@
         joined = jnp.concatenate([jnp.concatenate(outs, axis=0), value], axis=1)
         return jnp.dot(joined, weight, preferred_element_type=jnp.float32)
 
+    last[...] = jnp.zeros_like(last)
+
+    def readout_of(index):
+        c = index // peers
+        j = index % peers
+        row = lax.dot_general(
+            read, last[...], (((1,), (1,)), ((), ())), preferred_element_type=jnp.float32
+        )
+        for s in range(chunk):
+            pred[j, pl.ds(c * chunk + s, 1), :] = row[0:1, s * steps:(s + 1) * steps]
+
     def step(index, carry):
         c = index // peers
         j = index % peers
         feature_arrival(c, j).wait_recv()
+        readout_of((index + chunks * peers - 1) % (chunks * peers))
         hidden = recv[c, j].reshape(chunk * steps, channels)
         for layer in range(layers):
             dist = dil_ref[layer]
             inner = jnp.maximum(conv(hidden, lead_ref[layer], 2 * layer, j, dist), 0.0).astype(jnp.bfloat16)
             branch = jnp.maximum(conv(inner, trail_ref[layer], 2 * layer + 1, j, dist), 0.0)
             hidden = (hidden.astype(jnp.float32) + branch).astype(jnp.bfloat16)
-        for s in range(chunk):
-            row = lax.dot_general(
-                read, hidden[s * steps:(s + 1) * steps], (((1,), (1,)), ((), ())),
-                preferred_element_type=jnp.float32,
-            )
-            pred[j, pl.ds(c * chunk + s, 1), :] = row[0:1, :]
+        last[...] = hidden
         return carry
 
     lax.fori_loop(0, chunks * peers, step, 0)
+    readout_of(chunks * peers - 1)
 
     def pred_copy(k, s):
         to = lax.rem(me + k, peers)
@@ -329,6 +337,7 @@
         scratch_shapes=[
             pltpu.VMEM((chunks, peers, chunk, steps, channels), jnp.bfloat16),
             pltpu.VMEM((2 * layers, chunk, DMAX + peers * steps, channels), jnp.float32),
+            pltpu.VMEM((chunk * steps, channels), jnp.bfloat16),
             pltpu.VMEM((peers, per, steps), jnp.float32),
             pltpu.VMEM((peers * sides, per, steps), jnp.float32),
             pltpu.VMEM((own, steps), jnp.float32),

time: 137 us -> 136 us (level)
    pallas_call x1, Pallas kernels: 127 us -> 126 us  [sensor_form(): pl.pallas_call(functools.partial(exchange_kernel, peers, sides, chunk, ra...]
where the time goes in v4:
time: 136 us
  Pallas kernels  136 us (100%)
    pallas_call x1, Pallas kernels, sensor_form(): pl.pallas_call(functools.partial(exchange_kernel, peers, sides, chunk, ra...  126 us
    pallas_call x1, Pallas kernels, sensor_form(): pl.pallas_call(functools.partial(finish_kernel, own), out_shape=jax.Shape...  9.84 us

profile of v4, /device:TPU:0, one launch (start us, length us, event | category | flops | bytes accessed | tf_op | source)
XLA Modules:
  0.0 135.6 jit_solution(9544627402072074227)
XLA Ops:
  0.0 125.8 %exchange.1 = (f32[128,256]{1,0:T(8,128)}, f32[8,16,192]{2,1,0:T(8,128)}) custom-call(s32[3]{0:T(128)} %dil_ref.1, bf16[64,256,128]{2,1,0:T(8,128)(2,1)} %x_ref.1, f32[64,256]{1,0:T(8,128)} %tgt_ref.1, f32[64,256]{1,0:T(8,128)} %bitcast.6, bf16[3,256,128]{2,1,0:T(8,128)(2,1)} %bitcast.4, bf16[3,256,128]{2,1,0:T(8,128)(2,1)} %bitcast.5, bf16[1,128]{1,0:T(2,128)(2,1)} %bitcast.7), custom_call_target="tpu_custom_call" | custom-call | tf_op jit(solution)/shard_map/exchange/pallas_call | solution.py:326
  125.8 9.8 %finish.1 = f32[64,256]{1,0:T(8,128)} custom-call(f32[128,256]{1,0:T(8,128)} %get-tuple-element.7.resid_ref, f32[8,16,192]{2,1,0:T(8,128)} %get-tuple-element.8.total_ref), custom_call_target="tpu_custom_call" | custom-call | tf_op jit(solution)/shard_map/finish/pallas_call | solution.py:357
